TPU v7x, 32 devices: a whole 2x2x4 slice. The times are simulated.
32 devices in a mesh: slide: 2 (over y), tile: 16 (over z, x, core).
Axes of the slice: x: 2, y: 2, z: 4, core: 2. Of those that a mesh axis runs over, the one named last changes fastest.
Arguments:
- fine_level: bfloat16 [2, 128, 256, 256], P('slide', 'tile'), may hold values from -6 to 6
- coarse_level: bfloat16 [2, 64, 128, 256], P('slide', 'tile'), may hold values from -6 to 6
- fine_kernel: bfloat16 [256, 9, 128], replicated, may hold values from -0.125 to 0.125
- coarse_kernel: bfloat16 [256, 9, 128], replicated, may hold values from -0.125 to 0.125
- fine_gain: float32 [128], replicated, may hold values from 0.25 to 1.75
- fine_offset: float32 [128], replicated, may hold values from -3 to 3
- coarse_gain: float32 [128], replicated, may hold values from 0.25 to 1.75
- coarse_offset: float32 [128], replicated, may hold values from -3 to 3
- class_kernel: bfloat16 [8, 128], replicated
- class_offset: float32 [8], replicated, may hold values from -4 to 4
- tissue_labels: int32 [2, 128, 256], P('slide', 'tile'), may hold values from -1 to 7, as said below
Outputs:
- loss: float32 [], replicated
- head_grads: float32 [12, 128], replicated
- conv_grads: float32 [256, 2, 9, 128], P('tile')
Inputs may be any that keep to these rules, and one draw needn't show every extreme that they name: `tissue_labels`: -1 marks a pixel without tissue, other values are classes.
All inputs are finite; a program needn't handle non-finite values.
Results may differ from a plain program's by a relative error of at most 0.0033.
Values may be sent and summed in bfloat16 or wider, within the bound.
A program may use at most 128 MiB of HBM per device.

v0:
```python
import jax
import jax.numpy as jnp
from jax import lax
from jax.sharding import PartitionSpec as P

GROUPS = 32


epsilon = 1e-05


def padded_2(cells, sides, width):
    for axis, dim in sides:
        count = lax.axis_size(axis)
        ends = count - 1
        head = lax.slice_in_dim(cells, 0, width, axis=dim)
        tail = lax.slice_in_dim(cells, cells.shape[dim] - width, cells.shape[dim], axis=dim)
        cells = jnp.concatenate(
            [
                lax.ppermute(tail, axis, [(i, (i + 1) % count) for i in range(ends)]),
                cells,
                lax.ppermute(head, axis, [((i + 1) % count, i) for i in range(ends)]),
            ],
            axis=dim,
        )
    return cells


def shifted(padded, height, width, position):
    row_step = position // 3
    col_step = position % 3
    return padded[row_step : row_step + height, col_step : col_step + width].reshape(
        height * width, -1
    )


def convolve(padded, kernel, height, width):
    total = jnp.zeros((height * width, kernel.shape[2]), jnp.float32)
    for position in range(9):
        total = total + jnp.dot(
            shifted(padded, height, width, position),
            kernel[:, position, :],
            preferred_element_type=jnp.float32,
        )
    return total


def group_sums(values, groups):
    return values.reshape(values.shape[0], groups, -1).sum(axis=(0, 2))


def spread(per_group, channels):
    return jnp.repeat(per_group, channels // per_group.shape[0])


def per_device(
    fine_level,
    coarse_level,
    fine_kernel,
    coarse_kernel,
    fine_gain,
    fine_offset,
    coarse_gain,
    coarse_offset,
    class_kernel,
    class_offset,
    tissue_labels,
):
    tiles = lax.axis_size("tile")
    channels = fine_kernel.shape[2]
    in_channels = fine_kernel.shape[0]
    height, width = (fine_level.shape[1], fine_level.shape[2])
    labels = tissue_labels[0].reshape(-1)
    tissue = (labels >= 0).astype(jnp.float32)
    total = lax.psum(jnp.sum(tissue), ("slide", "tile"))
    fine_rows = padded_2(fine_level[0], (("tile", 0),), 1)
    coarse_rows = padded_2(coarse_level[0], (("tile", 0),), 1)
    fine_pad = jnp.pad(fine_rows, ((0, 0), (1, 1), (0, 0)))
    coarse_pad = jnp.pad(coarse_rows, ((0, 0), (1, 1), (0, 0)))
    fine_conv = convolve(fine_pad, fine_kernel, height, width)
    coarse_conv = convolve(coarse_pad, coarse_kernel, height // 2, width // 2)
    stats = lax.psum(
        (
            group_sums(fine_conv, GROUPS),
            group_sums(fine_conv * fine_conv, GROUPS),
            group_sums(coarse_conv, GROUPS),
            group_sums(coarse_conv * coarse_conv, GROUPS),
        ),
        "tile",
    )
    fine_number = height * tiles * width * (channels // GROUPS)
    coarse_number = fine_number // 4

    def normalize(conv_out, first_sum, square_sum, number, gain, offset):
        mean = first_sum / number
        variance = square_sum / number - mean * mean
        scale = spread(lax.rsqrt(variance + epsilon), channels)
        normed = (conv_out - spread(mean, channels)) * scale
        return (normed, scale, normed * gain + offset)

    fine_normed, fine_scale, fine_pre = normalize(
        fine_conv, stats[0], stats[1], fine_number, fine_gain, fine_offset
    )
    coarse_normed, coarse_scale, coarse_pre = normalize(
        coarse_conv, stats[2], stats[3], coarse_number, coarse_gain, coarse_offset
    )
    act_coarse = jnp.maximum(coarse_pre, 0.0).reshape(height // 2, width // 2, channels)
    upsampled = jnp.repeat(jnp.repeat(act_coarse, 2, 0), 2, 1).reshape(height * width, channels)
    merged = (jnp.maximum(fine_pre, 0.0) + upsampled).astype(jnp.bfloat16)
    logits = (
        lax.dot_general(
            class_kernel, merged, (((1,), (1,)), ((), ())), preferred_element_type=jnp.float32
        )
        + class_offset[:, None]
    )
    onehot = (
        labels[None, :] == jnp.arange(class_kernel.shape[0], dtype=jnp.int32)[:, None]
    ).astype(jnp.float32)
    top = jnp.max(logits, axis=0)
    lse = top + jnp.log(jnp.sum(jnp.exp(logits - top[None, :]), axis=0))
    loss_local = jnp.sum((lse - jnp.sum(onehot * logits, axis=0)) * tissue)
    dlogits = ((jnp.exp(logits - lse[None, :]) - onehot) * tissue[None, :] / total).astype(
        jnp.bfloat16
    )
    class_grad = jnp.dot(dlogits, merged, preferred_element_type=jnp.float32)
    dmerged = lax.dot_general(
        dlogits, class_kernel, (((0,), (0,)), ((), ())), preferred_element_type=jnp.float32
    )
    dact_coarse = (
        dmerged.reshape(height // 2, 2, width // 2, 2, channels)
        .sum(axis=(1, 3))
        .reshape(-1, channels)
    )
    fine_dpre = dmerged * (fine_pre > 0).astype(jnp.float32)
    coarse_dpre = dact_coarse * (coarse_pre > 0).astype(jnp.float32)
    fine_dnorm = fine_dpre * fine_gain
    coarse_dnorm = coarse_dpre * coarse_gain
    back = lax.psum(
        (
            group_sums(fine_dnorm, GROUPS),
            group_sums(fine_dnorm * fine_normed, GROUPS),
            group_sums(coarse_dnorm, GROUPS),
            group_sums(coarse_dnorm * coarse_normed, GROUPS),
        ),
        "tile",
    )
    fine_dconv = (
        (
            fine_dnorm
            - spread(back[0] / fine_number, channels)
            - fine_normed * spread(back[1] / fine_number, channels)
        )
        * fine_scale
    ).astype(jnp.bfloat16)
    coarse_dconv = (
        (
            coarse_dnorm
            - spread(back[2] / coarse_number, channels)
            - coarse_normed * spread(back[3] / coarse_number, channels)
        )
        * coarse_scale
    ).astype(jnp.bfloat16)
    head_local = jnp.concatenate(
        [
            jnp.stack(
                [
                    jnp.sum(fine_dpre * fine_normed, axis=0),
                    jnp.sum(fine_dpre, axis=0),
                    jnp.sum(coarse_dpre * coarse_normed, axis=0),
                    jnp.sum(coarse_dpre, axis=0),
                ],
                0,
            ),
            class_grad,
        ],
        0,
    )
    head_grads, loss_total = lax.psum((head_local, loss_local), ("slide", "tile"))
    sections = []
    for padded, upstream, rows_here, cols_here in (
        (fine_pad, fine_dconv, height, width),
        (coarse_pad, coarse_dconv, height // 2, width // 2),
    ):
        stacked = jnp.concatenate(
            [shifted(padded, rows_here, cols_here, position) for position in range(9)], 1
        )
        product = lax.dot_general(
            stacked, upstream, (((0,), (0,)), ((), ())), preferred_element_type=jnp.float32
        )
        sections.append(product.reshape(9, in_channels, channels).transpose(1, 0, 2))
    whole = lax.psum(jnp.stack(sections, 1), "slide")
    conv_grads = lax.psum_scatter(whole, "tile", scatter_dimension=0, tiled=True)
    return (loss_total / total, head_grads, conv_grads)


def solution(mesh):
    return jax.shard_map(
        per_device,
        mesh=mesh,
        in_specs=(
            P("slide", "tile", None, None),
            P("slide", "tile", None, None),
            P(),
            P(),
            P(),
            P(),
            P(),
            P(),
            P(),
            P(),
            P("slide", "tile", None),
        ),
        out_specs=(P(), P(), P("tile", None, None, None)),
        check_vma=False,
    )
```

profile of v0, /device:TPU:0, one launch (start us, length us, event | category | flops | bytes accessed | tf_op | source)
XLA Modules:
  0.0 292.0 jit_solution(8008616227894665407)
XLA Ops:
  7.2 0.9 slice_bitcast_fusion.3
  8.1 2.4 collective-permute-start.2
  10.5 1.3 collective-permute-start.3
  11.8 1.0 slice_bitcast_fusion.1
  12.8 5.3 %collective-permute-start = (bf16[1,256,256]{2,1,0:T(8,128)(2,1)S(1)}, bf16[1,256,256]{2,1,0:T(8,128)(2,1)S(1)}, u32[]{:S(2)}, u32[]{:S(2)}) collective-permute-start(bf16[1,256,256]{2,1,0:T(8,128)(2,1)S(1)} %get-tuple-element.43), channel_id=1, source_target_pairs={{0,1},{1,2},{2,3},{3,4},{4,5},{5,6},{6,7},{7,8},{8,9},{9,10},{10,1... | collective-permute-start | bytes 393224 | tf_op jit(solution)/shard_map/ppermute | solution.py:20
  18.1 1.3 collective-permute-start.1
  19.4 0.7 copy.17
  20.1 0.6 compare_convert_fusion
  20.7 1.1 fusion.19
  22.0 0.7 constant_dynamic-update-slice_fusion.17
  23.5 0.8 constant_dynamic-update-slice_fusion.16
  24.5 0.8 constant_dynamic-update-slice_fusion.15
  25.5 0.8 constant_dynamic-update-slice_fusion.14
  26.5 0.8 constant_dynamic-update-slice_fusion.13
  27.5 0.8 constant_dynamic-update-slice_fusion.12
  28.4 0.8 constant_dynamic-update-slice_fusion.11
  29.5 0.7 constant_dynamic-update-slice_fusion.10
  30.5 0.6 reduce_sum.217
  31.1 0.6 reduce_sum.220
  31.7 0.8 constant_dynamic-update-slice_fusion.9
  32.5 0.7 copy-done.20
  33.5 0.7 fusion.83
  34.2 1.3 constant_dynamic-update-slice_fusion.8
  39.5 1.6 fusion.80
  41.6 34.9 %all-reduce.4 = (f32[32]{0:T(128)S(1)}, f32[32]{0:T(128)S(1)}, f32[32]{0:T(128)S(1)}, f32[32]{0:T(128)S(1)}) all-reduce(f32[32]{0:T(128)S(1)} %copy-done.30, f32[32]{0:T(128)S(1)} %copy-done.29, f32[32]{0:T(128)S(1)} %reduce_sum.178, f32[32]{0:T(128)S(1)} %reduce_sum.175), channel_id=1, replica_groups=mesh['slide'=2,'tile'=16] {'tile'}, use_global_device_ids=true, to_apply=%region_11.12 | all-reduce | flops 128 | bytes 1024 | tf_op jit(solution)/shard_map/psum | solution.py:82
  77.8 0.7 copy-done.14
  78.7 0.8 copy-done.12
  79.9 0.6 convert_reduce_fusion
  80.5 37.0 %psum.89 = f32[]{:T(128)} all-reduce(f32[]{:T(128)} %get-tuple-element.20), channel_id=1, replica_groups=mesh['slide'=2,'tile'=16] {'slide','tile'}, use_global_device_ids=true, to_apply=%region_18.19 | all-reduce | flops 1 | bytes 8 | tf_op jit(solution)/shard_map/psum | solution.py:75
  117.5 4.0 %multiply_reduce_fusion.3 = (f32[128]{0:T(128)S(1)}, f32[128]{0:T(128)}, f32[128]{0:T(128)}, f32[128]{0:T(128)S(1)}, f32[2048,128]{1,0:T(8,128)}) fusion(f32[128]{0:T(128)} %param.15, f32[128]{0:T(128)} %param.16, f32[128]{0:T(128)} %copy-done.25, f32[2048,128]{1,0:T(8,128)} %get-tuple-element.60, f32[128]{0:T(128)} %copy-done.27, ...), kind=kOutput, calls=%fused_computation.38 | convolution fusion | flops 7716352 | bytes 2193412 | tf_op jit(solution)/shard_map/dot_general | solution.py:126
  122.0 2.7 reduce_sum.227
  124.7 1.8 multiply_reduce_fusion.4
  126.9 32.5 %all-reduce.3 = (f32[32]{0:T(128)S(1)}, f32[32]{0:T(128)S(1)}, f32[32]{0:T(128)S(1)}, f32[32]{0:T(128)S(1)}) all-reduce(f32[32]{0:T(128)S(1)} %reduce_sum.241, f32[32]{0:T(128)S(1)} %reduce_sum.238, f32[32]{0:T(128)S(1)} %reduce_sum.235, f32[32]{0:T(128)S(1)} %reduce_sum.232), channel_id=1, replica_groups=mesh['slide'=2,'tile'=16] {'tile'}, use_global_device_ids=true, to_apply=%region_36.37 | all-reduce | flops 128 | bytes 1024 | tf_op jit(solution)/shard_map/psum | solution.py:138
  160.2 2.5 constant_dynamic-update-slice_fusion.7
  162.7 1.1 constant_dynamic-update-slice_fusion.6
  163.8 1.1 constant_dynamic-update-slice_fusion.5
  164.9 1.1 constant_dynamic-update-slice_fusion.4
  166.0 1.1 constant_dynamic-update-slice_fusion.3
  167.1 1.2 constant_dynamic-update-slice_fusion.2
  168.4 1.1 constant_dynamic-update-slice_fusion.1
  169.5 1.2 constant_dynamic-update-slice_fusion
  170.7 5.4 %fusion.9 = f32[2304,128]{1,0:T(8,128)S(1)} fusion(bf16[2048,2304]{1,0:T(8,128)(2,1)} %constant_dynamic-update-slice_fusion, f32[2048,128]{1,0:T(8,128)S(1)} %copy-done.15, f32[128]{0:T(128)S(1)} %mul.148, f32[128]{0:T(128)S(1)} %sub.99, f32[128]{0:T(128)S(1)} %copy-done.35, f32[128]{0:T(128)S(1)} %copy-done.26, f32[128]{0:T(128)S(1)} %copy-done.28, ...), kind=kOutput, calls=%fused_computation.40 | convolution fusion | flops 1211105280 | bytes 12717056 | tf_op jit(solution)/shard_map/dot_general | solution.py:187
  176.1 2.5 fusion.21
  178.6 1.6 pad_maximum_fusion
  180.3 59.6 %reduce-scatter.2.cloned.1.call-done = f32[16,2,9,128]{3,0,2,1:T(8,128)} async-done(((f32[256,2,9,128]{3,0,2,1:T(8,128)}), f32[16,2,9,128]{3,0,2,1:T(8,128)}) %reduce-scatter.2.cloned.1.call-update) | async-done | bytes 147472 | tf_op jit(solution)/shard_map/reduce_scatter | solution.py:192
  240.0 0.8 fusion.75
  240.9 40.0 %all-reduce.2 = (f32[]{:T(128)}, f32[12,128]{1,0:T(8,128)}) all-reduce(f32[]{:T(128)} %get-tuple-element.21, f32[12,128]{1,0:T(8,128)S(1)} %concatenate.33), channel_id=1, replica_groups=mesh['slide'=2,'tile'=16] {'slide','tile'}, use_global_device_ids=true, to_apply=%region_16.17 | all-reduce | flops 1537 | bytes 12296 | tf_op jit(solution)/shard_map/psum | solution.py:178
  282.3 1.6 copy.16
  (149 shorter events, 10.8 us)
Async XLA Ops:
  7.2 72.4 %copy-start = (bf16[8,128]{1,0:T(8,128)(2,1)S(1)}, bf16[8,128]{1,0:T(8,128)(2,1)}, u32[]{:S(2)}) copy-start(bf16[8,128]{1,0:T(8,128)(2,1)} %param.19) | copy-start | bytes 6148
  7.2 232.8 %reduce-scatter.2.cloned.1.call-start = ((), (), s32[]{:S(2)}) async-start(), calls=%async_computation.1 | async-start | bytes 2506752 | tf_op jit(solution)/shard_map/reduce_scatter | solution.py:192
  8.1 12.6 %collective-permute-start.2 = (bf16[1,128,256]{2,1,0:T(8,128)(2,1)S(1)}, bf16[1,128,256]{2,1,0:T(8,128)(2,1)S(1)}, u32[]{:S(2)}, u32[]{:S(2)}) collective-permute-start(bf16[1,128,256]{2,1,0:T(8,128)(2,1)S(1)} %get-tuple-element.53), channel_id=1, source_target_pairs={{0,1},{1,2},{2,3},{3,4},{4,5},{5,6},{6,7},{7,8},{8,9},{9,10},{10,1... | collective-permute-start | bytes 196616 | tf_op jit(solution)/shard_map/ppermute | solution.py:20
  10.5 10.2 %collective-permute-start.3 = (bf16[1,128,256]{2,1,0:T(8,128)(2,1)S(1)}, bf16[1,128,256]{2,1,0:T(8,128)(2,1)S(1)}, u32[]{:S(2)}, u32[]{:S(2)}) collective-permute-start(bf16[1,128,256]{2,1,0:T(8,128)(2,1)S(1)} %get-tuple-element.54), channel_id=1, source_target_pairs={{1,0},{2,1},{3,2},{4,3},{5,4},{6,5},{7,6},{8,7},{9,8},{10,9},{11,1... | collective-permute-start | bytes 196616 | tf_op jit(solution)/shard_map/ppermute | solution.py:22
  12.8 9.9 %copy-start.19 = (bf16[256,9,128]{2,0,1:T(8,128)(2,1)S(1)}, bf16[256,9,128]{2,0,1:T(8,128)(2,1)}, u32[]{:S(2)}) copy-start(bf16[256,9,128]{2,0,1:T(8,128)(2,1)} %param.14) | copy-start | bytes 1769476
  12.8 19.7 %collective-permute-start = (bf16[1,256,256]{2,1,0:T(8,128)(2,1)S(1)}, bf16[1,256,256]{2,1,0:T(8,128)(2,1)S(1)}, u32[]{:S(2)}, u32[]{:S(2)}) collective-permute-start(bf16[1,256,256]{2,1,0:T(8,128)(2,1)S(1)} %get-tuple-element.43), channel_id=1, source_target_pairs={{0,1},{1,2},{2,3},{3,4},{4,5},{5,6},{6,7},{7,8},{8,9},{9,10},{10,1... | collective-permute-start | bytes 393224 | tf_op jit(solution)/shard_map/ppermute | solution.py:20
  18.1 14.4 %collective-permute-start.1 = (bf16[1,256,256]{2,1,0:T(8,128)(2,1)S(1)}, bf16[1,256,256]{2,1,0:T(8,128)(2,1)S(1)}, u32[]{:S(2)}, u32[]{:S(2)}) collective-permute-start(bf16[1,256,256]{2,1,0:T(8,128)(2,1)S(1)} %get-tuple-element.44), channel_id=1, source_target_pairs={{1,0},{2,1},{3,2},{4,3},{5,4},{6,5},{7,6},{8,7},{9,8},{10,9},{11,1... | collective-permute-start | bytes 393224 | tf_op jit(solution)/shard_map/ppermute | solution.py:22
  21.8 1.4 copy-start.11
  27.2 5.9 %copy-start.1 = (bf16[1,8,256,256]{3,2,1,0:T(8,128)(2,1)S(1)}, bf16[1,8,256,256]{3,2,1,0:T(8,128)(2,1)}, u32[]{:S(2)}) copy-start(bf16[1,8,256,256]{3,2,1,0:T(8,128)(2,1)} %param.11) | copy-start | bytes 3145732
  32.5 0.7 copy-start.20
  33.5 2.0 copy-start.18
  34.2 2.2 copy-start.6
  34.2 2.9 %copy-start.4 = (bf16[8,256,256]{2,1,0:T(8,128)(2,1)}, bf16[8,256,256]{2,1,0:T(8,128)(2,1)S(1)}, u32[]{:S(2)}) copy-start(bf16[8,256,256]{2,1,0:T(8,128)(2,1)S(1)} %get-tuple-element.38) | copy-start | bytes 3145732
  34.2 3.5 %copy-start.2 = (bf16[8,256,256]{2,1,0:T(8,128)(2,1)}, bf16[8,256,256]{2,1,0:T(8,128)(2,1)S(1)}, u32[]{:S(2)}) copy-start(bf16[8,256,256]{2,1,0:T(8,128)(2,1)S(1)} %get-tuple-element.37) | copy-start | bytes 3145732
  35.5 1.0 copy-start.21
  36.7 1.0 copy-start.10
  36.7 2.8 copy-start.8
  39.5 2.1 copy-start.29
  39.5 2.1 copy-start.30
  39.5 37.7 %copy-start.24 = (f32[128]{0:T(128)S(1)}, f32[128]{0:T(128)}, u32[]{:S(2)}) copy-start(f32[128]{0:T(128)} %param.17) | copy-start | bytes 1540
  39.5 37.7 %copy-start.31 = (f32[128]{0:T(128)S(1)}, f32[128]{0:T(128)}, u32[]{:S(2)}) copy-start(f32[128]{0:T(128)} %param.18) | copy-start | bytes 1540
  41.1 36.7 %copy-start.32 = (f32[128]{0:T(128)S(1)}, f32[128]{0:T(128)}, u32[]{:S(2)}) copy-start(f32[128]{0:T(128)} %param.16) | copy-start | bytes 1540
  41.1 36.7 %copy-start.34 = (f32[128]{0:T(128)S(1)}, f32[128]{0:T(128)}, u32[]{:S(2)}) copy-start(f32[128]{0:T(128)} %param.15) | copy-start | bytes 1540
  77.0 1.7 copy-start.25
  77.2 1.5 copy-start.27
  77.2 1.2 copy-start.14
  77.3 2.2 copy-start.38
  77.4 2.5 copy-start.23
  77.4 40.1 %copy-start.22 = (f32[2048]{0:T(1024)S(1)}, f32[2048]{0:T(1024)}, u32[]{:S(2)}) copy-start(f32[2048]{0:T(1024)} %compare_convert_fusion) | copy-start | bytes 24580
  78.7 0.8 copy-start.12
  160.2 2.5 copy-start.5
  160.2 3.6 %copy-start.3 = (bf16[8,256,256]{2,1,0:T(8,128)(2,1)S(1)}, bf16[8,256,256]{2,1,0:T(8,128)(2,1)}, u32[]{:S(2)}) copy-start(bf16[8,256,256]{2,1,0:T(8,128)(2,1)} %copy-done.2) | copy-start | bytes 3145732
  166.0 2.3 copy-start.9
  167.1 2.4 copy-start.7
  168.3 2.4 copy-start.15
  168.3 2.4 copy-start.17
  168.3 2.4 copy-start.26
  168.3 2.4 copy-start.28
  168.3 2.3 copy-start.33
  168.3 2.3 copy-start.35
  170.7 5.4 %copy-start.16 = (f32[512,128]{1,0:T(8,128)S(1)}, f32[512,128]{1,0:T(8,128)}, u32[]{:S(2)}) copy-start(f32[512,128]{1,0:T(8,128)} %get-tuple-element.32) | copy-start | bytes 786436
  180.2 59.7 %copy-start.13 = (bf16[2048,128]{1,0:T(8,128)(2,1)S(1)}, bf16[2048,128]{1,0:T(8,128)(2,1)}, u32[]{:S(2)}) copy-start(bf16[2048,128]{1,0:T(8,128)(2,1)} %copy-done.12) | copy-start | bytes 1572868
  180.3 60.6 %copy-start.36 = (f32[128]{0:T(128)S(1)}, f32[128]{0:T(128)}, u32[]{:S(2)}) copy-start(f32[128]{0:T(128)} %get-tuple-element.7) | copy-start | bytes 1540
  180.3 60.6 %copy-start.37 = (f32[128]{0:T(128)S(1)}, f32[128]{0:T(128)}, u32[]{:S(2)}) copy-start(f32[128]{0:T(128)} %get-tuple-element.8) | copy-start | bytes 1540
  180.3 102.1 %all-reduce.7.cloned.1.call-start = ((), (), s32[]{:S(2)}) async-start(), calls=%async_computation.2 | async-start | bytes 294912 | tf_op jit(solution)/shard_map/psum | solution.py:191
Sparse Core Ops, SparseCore 0:
  180.4 59.5 reduce-scatter.1
  242.2 20.6 all-reduce.6
where the time goes:
time: 293 us; the launch traced here: 292 us
  blocking collectives  144 us (49%)
  waiting for transfers between devices  59.7 us (20%)
  local copies, waits for them, and re-layouts  28.9 us (10%)
  matrix products  20 us (7%)
  between operations  17.2 us (6%)
  other arithmetic  11.3 us (4%)
  starting transfers between devices  10.3 us (4%)
    reduce_scatter x1, waiting for transfers between devices, per_device(): lax.psum_scatter(whole, 'tile', scatter_dimension=0, tiled=True)  59.6 us
    psum x1, blocking collectives, per_device(): lax.psum((head_local, loss_local), ('slide', 'tile'))  40 us
    psum x1, blocking collectives, per_device(): total = lax.psum(jnp.sum(tissue), ('slide', 'tile'))  37 us
    psum x1, blocking collectives, per_device(): lax.psum((group_sums(fine_conv, GROUPS), group_sums(fine_conv * fine_conv...  34.9 us
    psum x1, blocking collectives, per_device(): lax.psum((group_sums(fine_dnorm, GROUPS), group_sums(fine_dnorm * fine_no...  32.5 us
    unnamed x96, local copies, waits for them, and re-layouts  21.5 us
    dot_general x2, matrix products, per_device(): lax.dot_general(stacked, upstream, (((0,), (0,)), ((), ())), preferred_el...  7.89 us
    ppermute x2, starting transfers between devices, padded_2(): lax.ppermute(tail, axis, [(i, (i + 1) % count) for i in range(ends)])  7.66 us
  transfers between devices with their start and end apart: 6, of which 1 were waited for; matrix products, arithmetic and copies ran while one was open for 5% of the time, Pallas kernels for 0%

commit v1 on v0

v1 whole, which is shorter than its diff:
```python
import functools

import jax
import jax.numpy as jnp
from jax import lax
from jax.experimental import pallas as pl
from jax.experimental.pallas import tpu as pltpu
from jax.sharding import PartitionSpec as P

GROUPS = 32
EPSILON = 1e-05
F32 = jnp.float32
BF16 = jnp.bfloat16
MESH = pl.DeviceIdType.MESH
VMEM = pl.BlockSpec(memory_space=pltpu.VMEM)
LIMIT = 60 * 1024 * 1024
HIGH = lax.Precision.HIGHEST


def call(body, out_shape, scratch, args, collective_id=None):
    if collective_id is None:
        params = pltpu.CompilerParams(vmem_limit_bytes=LIMIT)
    else:
        params = pltpu.CompilerParams(
            vmem_limit_bytes=LIMIT, collective_id=collective_id, has_side_effects=True
        )
    return pl.pallas_call(
        body,
        out_shape=out_shape,
        in_specs=[VMEM] * len(args),
        out_specs=jax.tree.map(lambda _: VMEM, out_shape),
        scratch_shapes=scratch,
        compiler_params=params,
    )(*args)


def shape_of(dims, dtype=F32):
    return jax.ShapeDtypeStruct(dims, dtype)


def greet(peers):
    barrier = pltpu.get_barrier_semaphore()
    for peer in peers:
        pl.semaphore_signal(barrier, inc=1, device_id=peer, device_id_type=MESH)
    pl.semaphore_wait(barrier, len(peers))


def ring_peers(axis, size):
    me = lax.axis_index(axis)
    return [{axis: lax.rem(me + d, size)} for d in range(1, size)]


def spread_copies(axis, size, source, gather, send_sem, recv_sem):
    me = lax.axis_index(axis)
    return [
        pltpu.make_async_remote_copy(
            src_ref=source,
            dst_ref=gather.at[me],
            send_sem=send_sem.at[d - 1],
            recv_sem=recv_sem.at[d - 1],
            device_id={axis: lax.rem(me + d, size)},
            device_id_type=MESH,
        )
        for d in range(1, size)
    ]


def ordered_sum(gather, size):
    total = gather[0]
    for index in range(1, size):
        total = total + gather[index]
    return total


def dma_sems(*dims):
    return pltpu.SemaphoreType.DMA(dims)


def edge_kernel(tiles, fine, coarse, labels, fine_edge, coarse_edge, count_out,
                count, gather, down_send, down_recv, up_send, up_recv, send_sem, recv_sem):
    me = lax.axis_index("tile")
    tissue = (labels[...] >= 0).astype(F32)
    count[...] = jnp.broadcast_to(jnp.sum(tissue, axis=(0, 1), keepdims=True), count.shape)
    greet(ring_peers("tile", tiles))

    def edge_copies(peer, last, slot, send, recv):
        return [
            pltpu.make_async_remote_copy(
                src_ref=source.at[source.shape[0] - 1 if last else 0],
                dst_ref=target.at[slot],
                send_sem=send.at[at],
                recv_sem=recv.at[at],
                device_id={"tile": peer},
                device_id_type=MESH,
            )
            for at, (source, target) in enumerate(((fine, fine_edge), (coarse, coarse_edge)))
        ]

    down = edge_copies(lax.rem(me + 1, tiles), 1, 0, down_send, down_recv)
    up = edge_copies(lax.rem(me + tiles - 1, tiles), 0, 1, up_send, up_recv)

    @pl.when(me < tiles - 1)
    def _():
        for copy in down:
            copy.start()

    @pl.when(me > 0)
    def _():
        for copy in up:
            copy.start()

    copies = spread_copies("tile", tiles, count, gather, send_sem, recv_sem)
    for copy in copies:
        copy.start()
    gather[me] = count[...]

    @pl.when(me == 0)
    def _():
        fine_edge[0] = jnp.zeros(fine_edge.shape[1:], BF16)
        coarse_edge[0] = jnp.zeros(coarse_edge.shape[1:], BF16)

    @pl.when(me == tiles - 1)
    def _():
        fine_edge[1] = jnp.zeros(fine_edge.shape[1:], BF16)
        coarse_edge[1] = jnp.zeros(coarse_edge.shape[1:], BF16)

    for copy in copies:
        copy.wait()
    count_out[...] = ordered_sum(gather, tiles)

    @pl.when(me < tiles - 1)
    def _():
        for copy in down:
            copy.wait_send()
        for copy in up:
            copy.wait_recv()

    @pl.when(me > 0)
    def _():
        for copy in up:
            copy.wait_send()
        for copy in down:
            copy.wait_recv()


def pad_rows(level, edge, padded):
    rows = level.shape[0]
    padded[0] = edge[0]
    padded[pl.ds(1, rows)] = level[...]
    padded[rows + 1] = edge[1]


def column_of(shape, width):
    return lax.rem(lax.broadcasted_iota(jnp.int32, shape, 0), width)


def from_left(values, width):
    moved = pltpu.roll(values, 1, axis=0)
    return jnp.where(column_of(values.shape, width) == 0, 0.0, moved)


def from_right(values, width):
    moved = pltpu.roll(values, values.shape[0] - 1, axis=0)
    return jnp.where(column_of(values.shape, width) == width - 1, 0.0, moved)


def conv_kernel(fine, fine_edge, coarse, coarse_edge, fine_taps, coarse_taps,
                fine_conv, coarse_conv, stats, fine_pad, coarse_pad):
    pad_rows(fine, fine_edge, fine_pad)
    pad_rows(coarse, coarse_edge, coarse_pad)
    stats[...] = jnp.zeros_like(stats)
    for at, padded, taps, out in (
        (0, fine_pad, fine_taps, fine_conv),
        (2, coarse_pad, coarse_taps, coarse_conv),
    ):
        rows, width, depth = padded.shape[0] - 2, padded.shape[1], padded.shape[2]
        channels = taps.shape[2] // 3
        pack = 2
        size = pack * width

        @pl.loop(0, rows // pack)
        def _(step):
            total = None
            for a in range(3):
                block = padded[pl.ds(step * pack + a, pack)].reshape(size, depth)
                term = jnp.dot(block, taps[a], preferred_element_type=F32)
                total = term if total is None else total + term
            value = (
                from_left(total[:, :channels], width)
                + total[:, channels : 2 * channels]
                + from_right(total[:, 2 * channels :], width)
            )
            out[pl.ds(pl.multiple_of(step * size, size), size), :] = value
            stats[at : at + 1] += jnp.sum(value, axis=0, keepdims=True)
            stats[at + 1 : at + 2] += jnp.sum(value * value, axis=0, keepdims=True)


def stats_kernel(tiles, slides, local, count, out, total_out,
                 gather, count_gather, send_sem, recv_sem, slide_send, slide_recv):
    greet(ring_peers("tile", tiles) + ring_peers("slide", slides))
    copies = spread_copies("tile", tiles, local, gather, send_sem, recv_sem)
    others = spread_copies("slide", slides, count, count_gather, slide_send, slide_recv)
    for copy in copies + others:
        copy.start()
    gather[lax.axis_index("tile")] = local[...]
    count_gather[lax.axis_index("slide")] = count[...]
    for copy in copies + others:
        copy.wait()
    out[...] = ordered_sum(gather, tiles)
    total_out[...] = ordered_sum(count_gather, slides)


def group_total(rows, channels):
    width = channels // GROUPS
    first = lax.broadcasted_iota(jnp.int32, (channels, channels), 0) // width
    second = lax.broadcasted_iota(jnp.int32, (channels, channels), 1) // width
    same = (first == second).astype(F32)
    return jnp.dot(rows, same, preferred_element_type=F32, precision=HIGH)


def norm_terms(stats, numbers, channels):
    sums = group_total(stats[...], channels)
    terms = []
    for at, number in ((0, numbers[0]), (2, numbers[1])):
        mean = sums[at : at + 1] / number
        variance = sums[at + 1 : at + 2] / number - mean * mean
        terms.append((mean, lax.rsqrt(variance + EPSILON)))
    return terms


def head_kernel(numbers, width, fine_conv, coarse_conv, stats, norms, class_kernel,
                class_offset, labels, total, fine_dpre, coarse_dpre, rows, up, fold):
    channels = fine_conv.shape[1]
    classes = class_kernel.shape[0]
    (fine_mean, fine_scale), (coarse_mean, coarse_scale) = norm_terms(stats, numbers, channels)
    fine_gain, fine_offset = norms[0:1], norms[1:2]
    coarse_gain, coarse_offset = norms[2:3], norms[3:4]
    size, half = 2 * width, width // 2
    count = total[0:1, 0:1]
    rows[...] = jnp.zeros_like(rows)

    @pl.loop(0, fine_conv.shape[0] // size)
    def _(step):
        fine_at = pl.ds(pl.multiple_of(step * size, size), size)
        coarse_at = pl.ds(pl.multiple_of(step * half, half), half)
        fine_normed = (fine_conv[fine_at, :] - fine_mean) * fine_scale
        fine_pre = fine_normed * fine_gain + fine_offset
        coarse_normed = (coarse_conv[coarse_at, :] - coarse_mean) * coarse_scale
        coarse_pre = coarse_normed * coarse_gain + coarse_offset
        coarse_act = jnp.maximum(coarse_pre, 0.0)
        up[pl.ds(0, half, stride=2), :] = coarse_act
        up[pl.ds(1, half, stride=2), :] = coarse_act
        upsampled = up[...]
        merged = (
            jnp.maximum(fine_pre, 0.0) + jnp.concatenate([upsampled, upsampled], axis=0)
        ).astype(BF16)
        logits = (
            lax.dot_general(
                class_kernel[...], merged, (((1,), (1,)), ((), ())), preferred_element_type=F32
            )
            + class_offset[...]
        )
        label = labels[step]
        classes_of = lax.broadcasted_iota(jnp.int32, (classes, size), 0)
        onehot = (classes_of == label).astype(F32)
        tissue = (label >= 0).astype(F32)
        top = jnp.max(logits, axis=0, keepdims=True)
        lse = top + jnp.log(jnp.sum(jnp.exp(logits - top), axis=0, keepdims=True))
        picked = jnp.sum(onehot * logits, axis=0, keepdims=True)
        loss = jnp.sum((lse - picked) * tissue, axis=1, keepdims=True)
        dlogits = ((jnp.exp(logits - lse) - onehot) * tissue / count).astype(BF16)
        dmerged = lax.dot_general(
            dlogits, class_kernel[...], (((0,), (0,)), ((), ())), preferred_element_type=F32
        )
        fine_d = jnp.where(fine_pre > 0, dmerged, 0.0)
        fine_dpre[fine_at, :] = fine_d
        fold[...] = dmerged[:width] + dmerged[width:]
        blocks = fold[pl.ds(0, half, stride=2), :] + fold[pl.ds(1, half, stride=2), :]
        coarse_d = jnp.where(coarse_pre > 0, blocks, 0.0)
        coarse_dpre[coarse_at, :] = coarse_d
        rows[0:1] += jnp.sum(fine_d * fine_normed, axis=0, keepdims=True)
        rows[1:2] += jnp.sum(fine_d, axis=0, keepdims=True)
        rows[2:3] += jnp.sum(coarse_d * coarse_normed, axis=0, keepdims=True)
        rows[3:4] += jnp.sum(coarse_d, axis=0, keepdims=True)
        rows[4 : 4 + classes] += jnp.dot(dlogits, merged, preferred_element_type=F32)
        rows[4 + classes : 5 + classes] += jnp.broadcast_to(loss, (1, channels))


def rows_kernel(tiles, local, out, gather, send_sem, recv_sem):
    greet(ring_peers("tile", tiles))
    copies = spread_copies("tile", tiles, local, gather, send_sem, recv_sem)
    for copy in copies:
        copy.start()
    gather[lax.axis_index("tile")] = local[...]
    for copy in copies:
        copy.wait()
    out[...] = ordered_sum(gather, tiles)


def grad_kernel(numbers, fine, fine_edge, coarse, coarse_edge, fine_conv, coarse_conv, stats,
                norms, rows, fine_dpre, coarse_dpre, fine_out, coarse_out, fine_pad, coarse_pad):
    channels = fine_conv.shape[1]
    terms = norm_terms(stats, numbers, channels)
    pad_rows(fine, fine_edge, fine_pad)
    pad_rows(coarse, coarse_edge, coarse_pad)
    gains = jnp.concatenate([norms[0:1], norms[0:1], norms[2:3], norms[2:3]], axis=0)
    back = group_total(
        jnp.concatenate([rows[0:4] * gains, jnp.zeros((4, channels), F32)], axis=0), channels
    )
    for at, padded, conv, dpre, out in (
        (2, coarse_pad, coarse_conv, coarse_dpre, coarse_out),
        (0, fine_pad, fine_conv, fine_dpre, fine_out),
    ):
        number = numbers[at // 2]
        mean, scale = terms[at // 2]
        gain = norms[at : at + 1]
        first = back[at + 1 : at + 2] / number
        second = back[at : at + 1] / number
        height, width, depth = padded.shape[0] - 2, padded.shape[1], padded.shape[2]
        pack = 2
        size = pack * width
        out[...] = jnp.zeros_like(out)
        lead = out.shape[:-1]

        @pl.loop(0, height // pack)
        def _(step):
            here = pl.ds(pl.multiple_of(step * size, size), size)
            normed = (conv[here, :] - mean) * scale
            dconv = (dpre[here, :] * gain - first - normed * second) * scale
            moved = jnp.concatenate(
                [
                    from_right(dconv, width).astype(BF16),
                    dconv.astype(BF16),
                    from_left(dconv, width).astype(BF16),
                ],
                axis=1,
            )
            for a in range(3):
                block = padded[pl.ds(step * pack + a, pack)].reshape(size, depth)
                term = lax.dot_general(
                    block, moved, (((0,), (0,)), ((), ())), preferred_element_type=F32
                )
                at_lanes = (slice(None),) * len(lead) + (
                    slice(a * 3 * channels, (a + 1) * 3 * channels),
                )
                out[at_lanes] += term.reshape(lead + (3 * channels,))


def orders_of(bits):
    first = list(range(bits))
    second = list(first)
    if bits > 2:
        second[1], second[2] = second[2], second[1]
    return first, second


def stage_plan(bits, order):
    left = list(reversed(range(bits)))
    plan = []
    for bit in order:
        place = left.index(bit)
        left = [other for other in left if other != bit]
        plan.append((bit, place, len(left)))
    return plan


def at_bits(places, count):
    index = [slice(None)] * count
    for place, value in places:
        index[place] = value
    return tuple(index)


def scatter_kernel(bits, slides, channels, *refs):
    fine, coarse, rows, out, head = refs[:5]
    fine_bufs = refs[5 : 5 + 3 * bits]
    coarse_bufs = refs[5 + 3 * bits : 5 + 6 * bits]
    (final, head_gather, send_sem, recv_sem, slide_send, slide_recv) = refs[5 + 6 * bits :]
    me, slide = lax.axis_index("tile"), lax.axis_index("slide")
    mine = [lax.rem(me // (2**bit), 2) for bit in range(bits)]
    partners = [{"tile": me + (1 - 2 * mine[bit]) * (2**bit)} for bit in range(bits)]
    greet(partners + ring_peers("slide", slides))
    plans = [stage_plan(bits, order) for order in orders_of(bits)]
    bufs = [fine_bufs, coarse_bufs]

    heads = spread_copies("slide", slides, rows, head_gather, slide_send.at[2], slide_recv.at[2])
    for copy in heads:
        copy.start()

    def stage_copy(level, stage):
        bit, place, left = plans[level][stage]
        if stage == 0:
            source = (fine, coarse)[level].at[at_bits([(place, 1 - mine[bit])], left + 1)]
        else:
            source = bufs[level][3 * stage + 1]
        return pltpu.make_async_remote_copy(
            src_ref=source,
            dst_ref=bufs[level][3 * stage + 2],
            send_sem=send_sem.at[level, stage],
            recv_sem=recv_sem.at[level, stage],
            device_id=partners[bit],
            device_id_type=MESH,
        )

    def slide_copies(level):
        return spread_copies(
            "slide", slides, final.at[level, slide], final.at[level],
            slide_send.at[level], slide_recv.at[level],
        )

    both = (1, 0)
    for level in both:
        stage_copy(level, 0).start()
    for stage in range(bits):
        for level in both:
            bit, place, left = plans[level][stage]
            stage_copy(level, stage).wait()
            if stage == 0:
                kept = (fine, coarse)[level].at[at_bits([(place, mine[bit])], left + 1)]
            else:
                kept = bufs[level][3 * stage]
            came = bufs[level][3 * stage + 2]
            if stage == bits - 1:
                final[level, slide] = kept[...] + came[...].astype(F32)
                for copy in slide_copies(level):
                    copy.start()
                continue
            later, spot, _ = plans[level][stage + 1]

            def part(value):
                chosen = at_bits([(spot, value)], left)
                return kept[chosen] + came[chosen].astype(F32)

            outgoing = bufs[level][3 * stage + 4]
            outgoing[...] = part(1 - mine[later]).astype(outgoing.dtype)
            stage_copy(level, stage + 1).start()
            bufs[level][3 * stage + 3][...] = part(mine[later])

    head_gather[slide] = rows[...]
    for copy in heads:
        copy.wait()
    head[...] = ordered_sum(head_gather, slides)
    for level in both:
        for copy in slide_copies(level):
            copy.wait()
        whole = final[level, 0]
        for index in range(1, slides):
            whole = whole + final[level, index]
        for tap in range(9):
            out[:, level, tap, :] = whole[:, tap * channels : (tap + 1) * channels]


def scatter_scratch(bits, slides, depth, width, rows_shape):
    scratch = []
    for order in orders_of(bits):
        for stage, (_, _, left) in enumerate(stage_plan(bits, order)):
            wire = F32 if stage == 0 else BF16
            below = (2,) * left + (depth, width)
            if stage == 0:
                tiny = (8, 128)
                scratch += [pltpu.VMEM(tiny, F32), pltpu.VMEM(tiny, F32)]
            else:
                scratch += [pltpu.VMEM(below, F32), pltpu.VMEM(below, wire)]
            scratch += [pltpu.VMEM(below, wire)]
    ends = max(slides - 1, 1)
    return scratch + [
        pltpu.VMEM((2, slides, depth, width), F32),
        pltpu.VMEM((slides,) + rows_shape, F32),
        dma_sems(2, bits),
        dma_sems(2, bits),
        dma_sems(3, ends),
        dma_sems(3, ends),
    ]


def per_device(
    fine_level,
    coarse_level,
    fine_kernel,
    coarse_kernel,
    fine_gain,
    fine_offset,
    coarse_gain,
    coarse_offset,
    class_kernel,
    class_offset,
    tissue_labels,
):
    tiles, slides = lax.axis_size("tile"), lax.axis_size("slide")
    bits = tiles.bit_length() - 1
    in_channels, _, channels = fine_kernel.shape
    classes = class_kernel.shape[0]
    fine, coarse, labels = fine_level[0], coarse_level[0], tissue_labels[0]
    height, width = fine.shape[0], fine.shape[1]
    fine_number = height * tiles * width * (channels // GROUPS)
    numbers = (float(fine_number), float(fine_number // 4))
    ends = tiles - 1

    def tap_rows(kernel):
        return kernel.reshape(in_channels, 3, 3 * channels).transpose(1, 0, 2)

    fine_edge, coarse_edge, count = call(
        functools.partial(edge_kernel, tiles),
        (
            shape_of((2,) + fine.shape[1:], BF16),
            shape_of((2,) + coarse.shape[1:], BF16),
            shape_of((1, channels)),
        ),
        [
            pltpu.VMEM((1, channels), F32),
            pltpu.VMEM((tiles, 1, channels), F32),
            dma_sems(2),
            dma_sems(2),
            dma_sems(2),
            dma_sems(2),
            dma_sems(ends),
            dma_sems(ends),
        ],
        (fine, coarse, labels),
        0,
    )
    pads = [
        pltpu.VMEM((height + 2, width, in_channels), BF16),
        pltpu.VMEM((height // 2 + 2, width // 2, in_channels), BF16),
    ]
    pixels = height * width
    fine_conv, coarse_conv, local = call(
        conv_kernel,
        (
            shape_of((pixels, channels)),
            shape_of((pixels // 4, channels)),
            shape_of((8, channels)),
        ),
        pads,
        (fine, fine_edge, coarse, coarse_edge, tap_rows(fine_kernel), tap_rows(coarse_kernel)),
    )
    stats, total = call(
        functools.partial(stats_kernel, tiles, slides),
        (shape_of((8, channels)), shape_of((1, channels))),
        [
            pltpu.VMEM((tiles, 8, channels), F32),
            pltpu.VMEM((slides, 1, channels), F32),
            dma_sems(ends),
            dma_sems(ends),
            dma_sems(max(slides - 1, 1)),
            dma_sems(max(slides - 1, 1)),
        ],
        (local, count),
        1,
    )
    norms = jnp.stack([fine_gain, fine_offset, coarse_gain, coarse_offset], 0)
    row_count = -(-(5 + classes) // 8) * 8
    fine_dpre, coarse_dpre, rows_local = call(
        functools.partial(head_kernel, numbers, width),
        (
            shape_of((pixels, channels)),
            shape_of((pixels // 4, channels)),
            shape_of((row_count, channels)),
        ),
        [pltpu.VMEM((width, channels), F32), pltpu.VMEM((width, channels), F32)],
        (
            fine_conv,
            coarse_conv,
            stats,
            norms,
            class_kernel,
            class_offset[:, None],
            labels.reshape(height // 2, 1, 2 * width),
            total,
        ),
    )
    rows = call(
        functools.partial(rows_kernel, tiles),
        shape_of((row_count, channels)),
        [pltpu.VMEM((tiles, row_count, channels), F32), dma_sems(ends), dma_sems(ends)],
        (rows_local,),
        2,
    )
    chunk = in_channels // tiles
    grads_shape = shape_of((2,) * bits + (chunk, 9 * channels))
    fine_grad, coarse_grad = call(
        functools.partial(grad_kernel, numbers),
        (grads_shape, grads_shape),
        pads,
        (
            fine,
            fine_edge,
            coarse,
            coarse_edge,
            fine_conv,
            coarse_conv,
            stats,
            norms,
            rows,
            fine_dpre,
            coarse_dpre,
        ),
    )
    conv_grads, head = call(
        functools.partial(scatter_kernel, bits, slides, channels),
        (shape_of((chunk, 2, 9, channels)), shape_of((row_count, channels))),
        scatter_scratch(bits, slides, chunk, 9 * channels, (row_count, channels)),
        (fine_grad, coarse_grad, rows),
        3,
    )
    return (head[4 + classes, 0] / total[0, 0], head[: 4 + classes], conv_grads)


def solution(mesh):
    return jax.shard_map(
        per_device,
        mesh=mesh,
        in_specs=(
            P("slide", "tile", None, None),
            P("slide", "tile", None, None),
            P(),
            P(),
            P(),
            P(),
            P(),
            P(),
            P(),
            P(),
            P("slide", "tile", None),
        ),
        out_specs=(P(), P(), P("tile", None, None, None)),
        check_vma=False,
    )
```

time: 293 us -> 86.4 us (0.29)
  blocking collectives: 144 us -> 0 us
  Pallas kernels: 0 us -> 72.6 us
  waiting for transfers between devices: 59.7 us -> 0 us
  matrix products: 20 us -> 0 us
  local copies, waits for them, and re-layouts: 28.9 us -> 9.43 us
  between operations: 17.2 us -> 2.53 us
  starting transfers between devices: 10.3 us -> 0 us
  other arithmetic: 11.3 us -> 1.35 us
    psum x4 -> x0, blocking collectives: 144 us -> none  [the longest x1 40 us: per_device(): lax.psum((head_local, loss_local), ('slide', 'tile'))]
    pallas_call x0 -> x7, Pallas kernels: none -> 72.6 us  [call(): pl.pallas_call(body, out_shape=out_shape, in_specs=[VMEM] * len(args), ou...]
    reduce_scatter x1 -> x0, waiting for transfers between devices: 59.6 us -> none  [per_device(): lax.psum_scatter(whole, 'tile', scatter_dimension=0, tiled=True)]
    dot_general x23 -> x0, matrix products: 20 us -> none  [the longest x2 7.89 us: per_device(): lax.dot_general(stacked, upstream, (((0,), (0,)), ((), ())), preferred_el...]
    unnamed x96 -> x10, local copies, waits for them, and re-layouts: 21.5 us -> 3.49 us
    ppermute x4 -> x0, starting transfers between devices: 10.2 us -> none  [the longest x2 7.66 us: padded_2(): lax.ppermute(tail, axis, [(i, (i + 1) % count) for i in range(ends)])]
    reduce_sum x12 -> x0, other arithmetic: 7.09 us -> none  [the longest x9 3.73 us: group_sums(): return values.reshape(values.shape[0], groups, -1).sum(axis=(0, 2))]
  transfers between devices with their start and end apart: 6 -> 0, of which waited for: 1 -> 0; matrix products, arithmetic and copies ran while one was open for 5% -> 0% of each run, Pallas kernels for 0% -> 0%
where the time goes in v1:
time: 86.4 us; the launch traced here: 85.9 us
  Pallas kernels  72.6 us (84%)
  local copies, waits for them, and re-layouts  9.43 us (11%)
  between operations  2.53 us (3%)
  other arithmetic  1.35 us (2%)
    pallas_call x7, Pallas kernels, call(): pl.pallas_call(body, out_shape=out_shape, in_specs=[VMEM] * len(args), ou...  72.6 us
    unnamed x10, local copies, waits for them, and re-layouts  3.49 us
    reshape x2, local copies, waits for them, and re-layouts, tap_rows(): return kernel.reshape(in_channels, 3, 3 * channels).transpose(1, 0, 2)  2.12 us

profile of v1, /device:TPU:0, one launch (start us, length us, event | category | flops | bytes accessed | tf_op | source)
XLA Modules:
  0.0 85.9 jit_solution(9537167697753615090)
XLA Ops:
  0.6 0.0 copy-start
  0.6 1.4 %pad_maximum_fusion.norms = f32[4,128]{1,0:T(4,128)} fusion(f32[1,128]{1,0:T(1,128)} %bitcast.29, f32[1,128]{1,0:T(1,128)} %bitcast.30, f32[1,128]{1,0:T(1,128)} %bitcast.31, f32[1,128]{1,0:T(1,128)} %bitcast.32), kind=kLoop, calls=%fused_computation | loop fusion | flops 1536 | bytes 4096 | tf_op jit(solution)/shard_map/stack | solution.py:551
  2.0 1.3 %copy.20.class_offset = f32[8,1]{1,0:T(8,128)} copy(f32[8,1]{0,1:T(1,128)} %bitcast.28) | data formatting | bytes 64 | tf_op jit(solution)/shard_map/broadcast_in_dim | solution.py:567
  3.3 1.3 %reshape_squeeze.3.labels = s32[4,1,512]{2,1,0:T(1,128)} reshape(s32[1,8,256]{2,1,0:T(8,128)} %param.21) | data formatting | bytes 16384 | tf_op jit(solution)/shard_map/reshape;squeeze | solution.py:568
  4.6 13.0 %shard_map.130 = (bf16[2,256,256]{2,1,0:T(8,128)(2,1)}, bf16[2,128,256]{2,1,0:T(8,128)(2,1)}, f32[1,128]{1,0:T(1,128)}) custom-call(bf16[8,256,256]{2,1,0:T(8,128)(2,1)} %bitcast.15, bf16[4,128,256]{2,1,0:T(8,128)(2,1)} %bitcast.22, s32[8,256]{1,0:T(8,128)} %bitcast.25), custom_call_target="tpu_custom_call" | custom-call | tf_op jit(solution)/shard_map/pallas_call | solution.py:27
  17.6 0.0 copy-done
  17.6 0.0 copy-start.1
  17.6 0.2 copy.16
  17.9 1.1 %copy.17 = bf16[256,3,384]{2,0,1:T(8,128)(2,1)} copy(bf16[256,3,384]{0,2,1:T(8,128)(2,1)S(1)} %bitcast.18) | data formatting | bytes 1179648 | tf_op jit(solution)/shard_map/reshape | solution.py:500
  18.9 0.0 copy-done.1
  18.9 0.2 copy.18
  19.2 1.1 %copy.19 = bf16[256,3,384]{2,0,1:T(8,128)(2,1)} copy(bf16[256,3,384]{0,2,1:T(8,128)(2,1)S(1)} %bitcast.19) | data formatting | bytes 1179648 | tf_op jit(solution)/shard_map/reshape | solution.py:500
  20.3 6.0 %shard_map.131 = (f32[2048,128]{1,0:T(8,128)}, f32[512,128]{1,0:T(8,128)}, f32[8,128]{1,0:T(8,128)}) custom-call(bf16[8,256,256]{2,1,0:T(8,128)(2,1)} %bitcast.16, bf16[2,256,256]{2,1,0:T(8,128)(2,1)} %get-tuple-element.18.fine_edge, bf16[4,128,256]{2,1,0:T(8,128)(2,1)} %bitcast.23, bf16[2,128,256]{2,1,0:T(8,128)(2,1)} %get-tuple-element.19.coarse_edge, ...), custom_call_target="tpu_custom_call" | custom-call | tf_op jit(solution)/shard_map/pallas_call | solution.py:27
  26.3 9.5 %shard_map.132 = (f32[8,128]{1,0:T(8,128)}, f32[1,128]{1,0:T(1,128)}) custom-call(f32[8,128]{1,0:T(8,128)} %get-tuple-element.22.local, f32[1,128]{1,0:T(1,128)} %get-tuple-element.23.count), custom_call_target="tpu_custom_call" | custom-call | tf_op jit(solution)/shard_map/pallas_call | solution.py:27
  35.8 4.7 %shard_map.133 = (f32[2048,128]{1,0:T(8,128)}, f32[512,128]{1,0:T(8,128)}, f32[16,128]{1,0:T(8,128)}) custom-call(f32[2048,128]{1,0:T(8,128)} %get-tuple-element.20.fine_conv, f32[512,128]{1,0:T(8,128)} %get-tuple-element.21.coarse_conv, f32[8,128]{1,0:T(8,128)} %get-tuple-element.24.stats, f32[4,128]{1,0:T(4,128)} %pad_maximum_fusion.norms, ...), custom_call_target="tpu_custom_call" | custom-call | tf_op jit(solution)/shard_map/pallas_call | solution.py:27
  40.5 8.2 %shard_map.134.rows.refs_2_ = f32[16,128]{1,0:T(8,128)} custom-call(f32[16,128]{1,0:T(8,128)} %get-tuple-element.26.local), custom_call_target="tpu_custom_call" | custom-call | tf_op jit(solution)/shard_map/pallas_call | solution.py:27
  48.7 7.1 %shard_map.135 = (f32[2,2,2,2,16,1152]{5,4,3,2,1,0:T(8,128)}, f32[2,2,2,2,16,1152]{5,4,3,2,1,0:T(8,128)}) custom-call(bf16[8,256,256]{2,1,0:T(8,128)(2,1)} %bitcast.17, bf16[2,256,256]{2,1,0:T(8,128)(2,1)} %get-tuple-element.18.fine_edge, bf16[4,128,256]{2,1,0:T(8,128)(2,1)} %bitcast.24, bf16[2,128,256]{2,1,0:T(8,128)(2,1)} %get-tuple-element.19.coarse_edge, ...), custom_call_target="tpu_custom_call" | custom-call | tf_op jit(solution)/shard_map/pallas_call | solution.py:27
  55.8 0.0 copy-start.2
  55.8 24.1 %shard_map.136 = (f32[16,2,9,128]{3,2,1,0:T(8,128)}, f32[16,128]{1,0:T(8,128)}) custom-call(f32[2,2,2,2,16,1152]{5,4,3,2,1,0:T(8,128)} %get-tuple-element.29.refs_0_, f32[2,2,2,2,16,1152]{5,4,3,2,1,0:T(8,128)} %get-tuple-element.30.refs_1_, f32[16,128]{1,0:T(8,128)} %shard_map.134.rows.refs_2_), custom_call_target="tpu_custom_call" | custom-call | tf_op jit(solution)/shard_map/pallas_call | solution.py:27
  79.9 1.2 %slice.9 = f32[1,1]{1,0:T(1,128)} slice(f32[16,128]{1,0:T(8,128)} %get-tuple-element.31), slice={[12:13], [0:1]} | slice | bytes 8 | tf_op jit(solution)/shard_map/slice | solution.py:606
  81.1 0.0 copy-done.2
  81.8 1.7 %copy.21 = f32[16,2,9,128]{3,1,2,0:T(2,128)} copy(f32[16,2,9,128]{3,2,1,0:T(8,128)} %get-tuple-element.38) | data formatting | bytes 294912
  83.5 1.3 %copy.23 = f32[12,128]{1,0:T(8,128)} copy(f32[12,128]{1,0:T(8,128)} %bitcast.26) | data formatting | bytes 12288
Async XLA Ops:
  0.6 17.0 %copy-start = (bf16[256,9,128]{2,0,1:T(8,128)(2,1)S(1)}, bf16[256,9,128]{2,0,1:T(8,128)(2,1)}, u32[]{:S(2)}) copy-start(bf16[256,9,128]{2,0,1:T(8,128)(2,1)} %param.13) | copy-start | bytes 1769476
  17.6 1.3 %copy-start.1 = (bf16[256,9,128]{2,0,1:T(8,128)(2,1)S(1)}, bf16[256,9,128]{2,0,1:T(8,128)(2,1)}, u32[]{:S(2)}) copy-start(bf16[256,9,128]{2,0,1:T(8,128)(2,1)} %param.14) | copy-start | bytes 1769476
  55.8 25.3 %copy-start.2 = (f32[1,128]{1,0:T(1,128)S(1)}, f32[1,128]{1,0:T(1,128)}, u32[]{:S(2)}) copy-start(f32[1,128]{1,0:T(1,128)} %get-tuple-element.25.total) | copy-start | bytes 1540

commit v2 on v0

v2 whole, which is shorter than its diff:
```python
import functools
import types

import jax
import jax.numpy as jnp
from jax import lax
from jax.experimental import pallas as pl
from jax.experimental.pallas import tpu as pltpu
from jax.sharding import PartitionSpec as P

GROUPS = 32
EPSILON = 1e-05
F32 = jnp.float32
BF16 = jnp.bfloat16
MESH = pl.DeviceIdType.MESH
VMEM = pl.BlockSpec(memory_space=pltpu.VMEM)
LIMIT = 60 * 1024 * 1024
HIGH = lax.Precision.HIGHEST


def call(body, out_shape, scratch, args, collective_id=None):
    if collective_id is None:
        params = pltpu.CompilerParams(vmem_limit_bytes=LIMIT)
    else:
        params = pltpu.CompilerParams(
            vmem_limit_bytes=LIMIT, collective_id=collective_id, has_side_effects=True
        )
    return pl.pallas_call(
        body,
        out_shape=out_shape,
        in_specs=[VMEM] * len(args),
        out_specs=jax.tree.map(lambda _: VMEM, out_shape),
        scratch_shapes=scratch,
        compiler_params=params,
    )(*args)


def shape_of(dims, dtype=F32):
    return jax.ShapeDtypeStruct(dims, dtype)


def greet(peers):
    barrier = pltpu.get_barrier_semaphore()
    for peer in peers:
        pl.semaphore_signal(barrier, inc=1, device_id=peer, device_id_type=MESH)
    pl.semaphore_wait(barrier, len(peers))


def ring_peers(axis, size):
    me = lax.axis_index(axis)
    return [{axis: lax.rem(me + d, size)} for d in range(1, size)]


def spread_copies(axis, size, source, gather, send_sem, recv_sem):
    me = lax.axis_index(axis)
    return [
        pltpu.make_async_remote_copy(
            src_ref=source,
            dst_ref=gather.at[me],
            send_sem=send_sem.at[d - 1],
            recv_sem=recv_sem.at[d - 1],
            device_id={axis: lax.rem(me + d, size)},
            device_id_type=MESH,
        )
        for d in range(1, size)
    ]


def ordered_sum(gather, size):
    total = gather[0]
    for index in range(1, size):
        total = total + gather[index]
    return total


def dma_sems(*dims):
    return pltpu.SemaphoreType.DMA(dims)


def column_of(shape, width):
    return lax.rem(lax.broadcasted_iota(jnp.int32, shape, 0), width)


def from_left(values, width):
    moved = pltpu.roll(values, 1, axis=0)
    return jnp.where(column_of(values.shape, width) == 0, 0.0, moved)


def from_right(values, width):
    moved = pltpu.roll(values, values.shape[0] - 1, axis=0)
    return jnp.where(column_of(values.shape, width) == width - 1, 0.0, moved)


def stage_plan(bits, order):
    left = list(reversed(range(bits)))
    plan = []
    for bit in order:
        place = left.index(bit)
        left = [other for other in left if other != bit]
        plan.append((bit, place, len(left)))
    return plan


def at_bits(places, count):
    index = [slice(None)] * count
    for place, value in places:
        index[place] = value
    return tuple(index)


def order_of(bits, turn):
    order = list(range(bits))
    if turn and bits > 2:
        order[1], order[2] = order[2], order[1]
    return order


def lanes_of(shape, dim=1):
    return lax.broadcasted_iota(jnp.int32, shape, dim)


def packed_groups(rows, channels):
    shape = (channels, channels)
    member = lanes_of(shape, 0) // (channels // GROUPS) == lax.rem(lanes_of(shape), GROUPS)
    sums = jnp.dot(rows, member.astype(F32), preferred_element_type=F32, precision=HIGH)
    own = lanes_of(rows.shape) // GROUPS == lanes_of(rows.shape, 0)
    return jnp.sum(jnp.where(own, sums, 0.0), axis=0, keepdims=True)


def unpacked_groups(row, channels):
    shape = (channels, channels)
    member = lax.rem(lanes_of(shape, 0), GROUPS) == lanes_of(shape) // (channels // GROUPS)
    own = lanes_of((8, channels)) // GROUPS == lanes_of((8, channels), 0)
    rows = jnp.where(own, jnp.broadcast_to(row, (8, channels)), 0.0)
    return jnp.dot(rows, member.astype(F32), preferred_element_type=F32, precision=HIGH)


PACK = 2
GRAD, SEND, RECV, KEPT = range(4)


def conv_step(step, padded, taps, out, sums, at):
    width, depth = padded.shape[1], padded.shape[2]
    channels = taps.shape[2]
    size = PACK * width
    total = None
    for a in range(3):
        block = padded[pl.ds(step * PACK + a, PACK)].reshape(size, depth)
        side = jnp.concatenate([taps[3 * a + b] for b in range(3)], axis=1)
        term = jnp.dot(block, side, preferred_element_type=F32)
        total = term if total is None else total + term
    value = (
        from_left(total[:, :channels], width)
        + total[:, channels : 2 * channels]
        + from_right(total[:, 2 * channels :], width)
    )
    here = step * size if isinstance(step, int) else pl.multiple_of(step * size, size)
    out[pl.ds(here, size), :] = value
    sums[at : at + 1] += jnp.sum(value, axis=0, keepdims=True)
    sums[at + 1 : at + 2] += jnp.sum(value * value, axis=0, keepdims=True)


def step_kernel(tiles, slides, bits, numbers, names, keys, *refs):
    ref = types.SimpleNamespace(**dict(zip(names, refs)))
    ref.parts = dict(zip(keys, refs[len(names) :]))
    fine, coarse, labels = ref.fine, ref.coarse, ref.labels
    fine_pad, coarse_pad = ref.fine_pad, ref.coarse_pad
    fine_conv, coarse_conv = ref.fine_conv, ref.coarse_conv
    sums, rows, class_kernel = ref.sums, ref.rows, ref.class_kernel
    me, slide = lax.axis_index("tile"), lax.axis_index("slide")
    height, width, _ = fine.shape
    channels = fine_conv.shape[1]
    classes = class_kernel.shape[0]
    fine_gain, fine_offset = ref.fine_gain[...], ref.fine_offset[...]
    coarse_gain, coarse_offset = ref.coarse_gain[...], ref.coarse_offset[...]

    tissue_here = (labels[...] >= 0).astype(F32)
    ref.count[...] = jnp.broadcast_to(
        jnp.sum(tissue_here, axis=(0, 1), keepdims=True), ref.count.shape
    )
    greet(ring_peers("tile", tiles) + ring_peers("slide", slides))

    def edge_copies(peer, down):
        return [
            pltpu.make_async_remote_copy(
                src_ref=source.at[source.shape[0] - 1 if down else 0],
                dst_ref=target.at[0 if down else target.shape[0] - 1],
                send_sem=ref.edge_send.at[int(down), at],
                recv_sem=ref.edge_recv.at[int(down), at],
                device_id={"tile": peer},
                device_id_type=MESH,
            )
            for at, (source, target) in enumerate(((fine, fine_pad), (coarse, coarse_pad)))
        ]

    down = edge_copies(lax.rem(me + 1, tiles), True)
    up = edge_copies(lax.rem(me + tiles - 1, tiles), False)

    @pl.when(me < tiles - 1)
    def _():
        for copy in down:
            copy.start()

    @pl.when(me > 0)
    def _():
        for copy in up:
            copy.start()

    def tile_copies(at, source, gather):
        return spread_copies(
            "tile", tiles, source, gather, ref.tile_send.at[at], ref.tile_recv.at[at]
        )

    def slide_copies(at, source, gather):
        return spread_copies(
            "slide", slides, source, gather, ref.slide_send.at[at], ref.slide_recv.at[at]
        )

    def start(copies):
        for copy in copies:
            copy.start()

    def wait(copies):
        for copy in copies:
            copy.wait()

    counts = tile_copies(0, ref.count, ref.count_gather)
    start(counts)
    ref.count_gather[me] = ref.count[...]

    @pl.when(me == 0)
    def _():
        for padded in (fine_pad, coarse_pad):
            padded[0] = jnp.zeros(padded.shape[1:], BF16)

    @pl.when(me == tiles - 1)
    def _():
        for padded in (fine_pad, coarse_pad):
            padded[padded.shape[0] - 1] = jnp.zeros(padded.shape[1:], BF16)

    sums[...] = jnp.zeros_like(sums)
    fine_pad[pl.ds(1, height)] = fine[...]
    coarse_pad[pl.ds(1, height // 2)] = coarse[...]
    fine_steps, coarse_steps = height // PACK, height // 2 // PACK

    @pl.loop(1, fine_steps - 1)
    def _(step):
        conv_step(step, fine_pad, ref.fine_taps, fine_conv, sums, 0)

    @pl.when(me < tiles - 1)
    def _():
        for copy in down:
            copy.wait_send()
        for copy in up:
            copy.wait_recv()

    @pl.when(me > 0)
    def _():
        for copy in up:
            copy.wait_send()
        for copy in down:
            copy.wait_recv()

    @pl.loop(0, 2)
    def _(side):
        conv_step(side * (fine_steps - 1), fine_pad, ref.fine_taps, fine_conv, sums, 0)

    @pl.loop(0, coarse_steps)
    def _(step):
        conv_step(step, coarse_pad, ref.coarse_taps, coarse_conv, sums, 2)

    ref.stat[...] = packed_groups(sums[...], channels)
    stat_copies = tile_copies(1, ref.stat, ref.stat_gather)
    start(stat_copies)
    wait(counts)
    ref.slide_count[...] = ordered_sum(ref.count_gather, tiles)
    total_copies = slide_copies(0, ref.slide_count, ref.total_gather)
    start(total_copies)
    ref.stat_gather[me] = ref.stat[...]
    ref.total_gather[slide] = ref.slide_count[...]

    for padded, turned in ((fine_pad, ref.fine_turned), (coarse_pad, ref.coarse_turned)):
        span = padded.shape[1]
        for row in range(padded.shape[0]):
            turned[:, row * span : (row + 1) * span] = padded[row].T

    wait(stat_copies)
    wait(total_copies)
    total = ordered_sum(ref.total_gather, slides)
    count = total[0:1, 0:1]
    ref.total_out[...] = total
    group_sums = unpacked_groups(ordered_sum(ref.stat_gather, tiles), channels)

    def terms_of(at, number):
        mean = group_sums[at : at + 1] / number
        variance = group_sums[at + 1 : at + 2] / number - mean * mean
        return mean, lax.rsqrt(variance + EPSILON)

    fine_mean, fine_scale = terms_of(0, numbers[0])
    coarse_mean, coarse_scale = terms_of(2, numbers[1])

    size, half = 2 * width, width // 2
    square = (classes, classes)
    offset = jnp.sum(
        jnp.where(
            lanes_of(square) == lanes_of(square, 0),
            jnp.broadcast_to(ref.class_offset[...], square),
            0.0,
        ),
        axis=1,
        keepdims=True,
    )
    rows[...] = jnp.zeros_like(rows)
    widen, fold = ref.widen, ref.fold
    fine_dpre, coarse_dpre = ref.fine_dpre, ref.coarse_dpre

    @pl.loop(0, height // 2)
    def _(step):
        fine_at = pl.ds(pl.multiple_of(step * size, size), size)
        coarse_at = pl.ds(pl.multiple_of(step * half, half), half)
        fine_normed = (fine_conv[fine_at, :] - fine_mean) * fine_scale
        fine_pre = fine_normed * fine_gain + fine_offset
        coarse_normed = (coarse_conv[coarse_at, :] - coarse_mean) * coarse_scale
        coarse_pre = coarse_normed * coarse_gain + coarse_offset
        coarse_act = jnp.maximum(coarse_pre, 0.0)
        widen[pl.ds(0, half, stride=2), :] = coarse_act
        widen[pl.ds(1, half, stride=2), :] = coarse_act
        upsampled = widen[...]
        merged = (
            jnp.maximum(fine_pre, 0.0) + jnp.concatenate([upsampled, upsampled], axis=0)
        ).astype(BF16)
        logits = (
            lax.dot_general(
                class_kernel[...], merged, (((1,), (1,)), ((), ())), preferred_element_type=F32
            )
            + offset
        )
        label = jnp.concatenate(
            [labels[pl.ds(2 * step, 1), :], labels[pl.ds(2 * step + 1, 1), :]], axis=1
        )
        onehot = (lanes_of((classes, size), 0) == label).astype(F32)
        tissue = (label >= 0).astype(F32)
        top = jnp.max(logits, axis=0, keepdims=True)
        lse = top + jnp.log(jnp.sum(jnp.exp(logits - top), axis=0, keepdims=True))
        picked = jnp.sum(onehot * logits, axis=0, keepdims=True)
        loss = jnp.sum((lse - picked) * tissue, axis=1, keepdims=True)
        dlogits = ((jnp.exp(logits - lse) - onehot) * tissue / count).astype(BF16)
        dmerged = lax.dot_general(
            dlogits, class_kernel[...], (((0,), (0,)), ((), ())), preferred_element_type=F32
        )
        fine_d = jnp.where(fine_pre > 0, dmerged, 0.0)
        fine_dpre[fine_at, :] = fine_d
        fold[...] = dmerged[:width] + dmerged[width:]
        blocks = fold[pl.ds(0, half, stride=2), :] + fold[pl.ds(1, half, stride=2), :]
        coarse_d = jnp.where(coarse_pre > 0, blocks, 0.0)
        coarse_dpre[coarse_at, :] = coarse_d
        rows[0:1] += jnp.sum(fine_d * fine_normed, axis=0, keepdims=True)
        rows[1:2] += jnp.sum(fine_d, axis=0, keepdims=True)
        rows[2:3] += jnp.sum(coarse_d * coarse_normed, axis=0, keepdims=True)
        rows[3:4] += jnp.sum(coarse_d, axis=0, keepdims=True)
        rows[4 : 4 + classes] += jnp.dot(dlogits, merged, preferred_element_type=F32)
        rows[4 + classes : 5 + classes] += jnp.broadcast_to(loss, (1, channels))

    gains = jnp.concatenate([fine_gain, fine_gain, coarse_gain, coarse_gain] * 2, axis=0)
    ref.back[...] = packed_groups(rows[0:8] * gains, channels)
    back_copies = tile_copies(2, ref.back, ref.back_gather)
    start(back_copies)
    row_copies = tile_copies(3, rows, ref.row_gather)
    start(row_copies)
    ref.back_gather[me] = ref.back[...]
    ref.row_gather[me] = rows[...]
    wait(back_copies)
    back = unpacked_groups(ordered_sum(ref.back_gather, tiles), channels)

    def upstream(conv, dpre, mean, scale, gain, at, number, span, shifted, steps):
        first = back[at + 1 : at + 2] / number
        second = back[at : at + 1] / number
        block = PACK * span

        @pl.loop(0, steps)
        def _(step):
            here = pl.ds(pl.multiple_of(step * block, block), block)
            normed = (conv[here, :] - mean) * scale
            dconv = (dpre[here, :] * gain - first - normed * second) * scale
            shifted[here, :] = jnp.concatenate(
                [
                    from_right(dconv, span).astype(BF16),
                    dconv.astype(BF16),
                    from_left(dconv, span).astype(BF16),
                ],
                axis=1,
            )

    mine = [lax.rem(me // (2**bit), 2) for bit in range(bits)]
    partners = [{"tile": me + (1 - 2 * mine[bit]) * (2**bit)} for bit in range(bits)]
    plans = [stage_plan(bits, order_of(bits, piece % 2 == 0)) for piece in range(4)]
    final = ref.final
    total_taps = 9 * channels
    spans = [(total_taps, total_taps)] + [(a * 3 * channels, 3 * channels) for a in range(3)]

    def buffer(piece, stage, kind):
        return ref.parts[kind, piece, stage]

    def stage_copy(piece, stage):
        bit, place, left = plans[piece][stage]
        if stage == 0:
            source = ref.parts[GRAD, piece, 0].at[at_bits([(place, 1 - mine[bit])], left + 1)]
        else:
            source = buffer(piece, stage, SEND)
        return pltpu.make_async_remote_copy(
            src_ref=source,
            dst_ref=buffer(piece, stage, RECV),
            send_sem=ref.stage_send.at[piece, stage],
            recv_sem=ref.stage_recv.at[piece, stage],
            device_id=partners[bit],
            device_id_type=MESH,
        )

    def piece_copies(piece):
        lanes = pl.ds(*spans[piece])
        return [
            pltpu.make_async_remote_copy(
                src_ref=final.at[slide, :, lanes],
                dst_ref=final.at[slide, :, lanes],
                send_sem=ref.slide_send.at[2 + piece, d - 1],
                recv_sem=ref.slide_recv.at[2 + piece, d - 1],
                device_id={"slide": lax.rem(slide + d, slides)},
                device_id_type=MESH,
            )
            for d in range(1, slides)
        ]

    done = [0] * 4

    def advance(piece):
        stage = done[piece]
        if stage == bits:
            return
        done[piece] += 1
        bit, place, left = plans[piece][stage]
        stage_copy(piece, stage).wait()
        if stage == 0:
            kept = ref.parts[GRAD, piece, 0].at[at_bits([(place, mine[bit])], left + 1)]
        else:
            kept = buffer(piece, stage, KEPT)
        came = buffer(piece, stage, RECV)
        if stage == bits - 1:
            final[slide, :, pl.ds(*spans[piece])] = kept[...] + came[...].astype(F32)
            start(piece_copies(piece))
            return
        later, spot, _ = plans[piece][stage + 1]

        def part(value):
            chosen = at_bits([(spot, value)], left)
            return kept[chosen] + came[chosen].astype(F32)

        buffer(piece, stage + 1, SEND)[...] = part(1 - mine[later]).astype(BF16)
        stage_copy(piece, stage + 1).start()
        buffer(piece, stage + 1, KEPT)[...] = part(mine[later])

    def product(turned, shifted, a, span):
        pixels = shifted.shape[0]
        return jnp.dot(
            turned[:, a * span : a * span + pixels], shifted[...], preferred_element_type=F32
        )

    coarse_shifted, fine_shifted = ref.coarse_shifted, ref.fine_shifted
    upstream(coarse_conv, coarse_dpre, coarse_mean, coarse_scale, coarse_gain, 2, numbers[1],
             half, coarse_shifted, coarse_steps)
    lead = (slice(None),) * (bits + 1)
    for a in range(3):
        value = product(ref.coarse_turned, coarse_shifted, a, half)
        out = ref.parts[GRAD, 0, 0]
        out[lead + (slice(a * 3 * channels, (a + 1) * 3 * channels),)] = value.reshape(
            out.shape[:-1] + (3 * channels,)
        )
    stage_copy(0, 0).start()
    upstream(fine_conv, fine_dpre, fine_mean, fine_scale, fine_gain, 0, numbers[0],
             width, fine_shifted, fine_steps)
    for a in range(3):
        out = ref.parts[GRAD, a + 1, 0]
        out[...] = product(ref.fine_turned, fine_shifted, a, width).reshape(out.shape)
        stage_copy(a + 1, 0).start()
        if a < 2:
            for piece in range(a + 1):
                advance(piece)
    wait(row_copies)
    ref.slide_rows[...] = ordered_sum(ref.row_gather, tiles)
    head_copies = slide_copies(1, ref.slide_rows, ref.head_gather)
    start(head_copies)
    ref.head_gather[slide] = ref.slide_rows[...]
    while min(done) < bits:
        for piece in range(4):
            advance(piece)
    wait(head_copies)
    for piece in range(4):
        wait(piece_copies(piece))


def finish_kernel(slides, classes, final, heads, total, loss, head, grads):
    channels = head.shape[1]
    whole = ordered_sum(final, slides)
    for level in range(2):
        for tap in range(9):
            at = (9 * level + tap) * channels
            grads[:, tap, level, :] = whole[:, at : at + channels]
    rows = ordered_sum(heads, slides)
    head[...] = rows[: 4 + classes]
    loss[...] = rows[4 + classes : 5 + classes, 0:1] / total[0:1, 0:1]


def per_device(
    fine_level,
    coarse_level,
    fine_kernel,
    coarse_kernel,
    fine_gain,
    fine_offset,
    coarse_gain,
    coarse_offset,
    class_kernel,
    class_offset,
    tissue_labels,
):
    tiles, slides = lax.axis_size("tile"), lax.axis_size("slide")
    bits = tiles.bit_length() - 1
    in_channels, _, channels = fine_kernel.shape
    classes = class_kernel.shape[0]
    fine, coarse, labels = fine_level[0], coarse_level[0], tissue_labels[0]
    height, width = fine.shape[0], fine.shape[1]
    fine_number = height * tiles * width * (channels // GROUPS)
    numbers = (float(fine_number), float(fine_number // 4))
    pixels, half = height * width, width // 2
    tile_ends, slide_ends = tiles - 1, max(slides - 1, 1)
    chunk = in_channels // tiles
    row_count = -(-(5 + classes) // 8) * 8

    inputs = dict(
        fine=fine,
        coarse=coarse,
        fine_taps=fine_kernel.transpose(1, 0, 2),
        coarse_taps=coarse_kernel.transpose(1, 0, 2),
        fine_gain=fine_gain[None, :],
        fine_offset=fine_offset[None, :],
        coarse_gain=coarse_gain[None, :],
        coarse_offset=coarse_offset[None, :],
        class_kernel=class_kernel,
        class_offset=class_offset[None, :],
        labels=labels,
    )
    outputs = dict(
        final=shape_of((slides, chunk, 18 * channels)),
        head_gather=shape_of((slides, row_count, channels)),
        total_out=shape_of((1, channels)),
    )
    line = (1, channels)
    scratch = dict(
        fine_pad=pltpu.VMEM((height + 2, width, in_channels), BF16),
        coarse_pad=pltpu.VMEM((height // 2 + 2, half, in_channels), BF16),
        fine_conv=pltpu.VMEM((pixels, channels), F32),
        coarse_conv=pltpu.VMEM((pixels // 4, channels), F32),
        fine_dpre=pltpu.VMEM((pixels, channels), F32),
        coarse_dpre=pltpu.VMEM((pixels // 4, channels), F32),
        fine_turned=pltpu.VMEM((in_channels, (height + 2) * width), BF16),
        coarse_turned=pltpu.VMEM((in_channels, (height // 2 + 2) * half), BF16),
        fine_shifted=pltpu.VMEM((pixels, 3 * channels), BF16),
        coarse_shifted=pltpu.VMEM((pixels // 4, 3 * channels), BF16),
        widen=pltpu.VMEM((width, channels), F32),
        fold=pltpu.VMEM((width, channels), F32),
        sums=pltpu.VMEM((8, channels), F32),
        rows=pltpu.VMEM((row_count, channels), F32),
        slide_rows=pltpu.VMEM((row_count, channels), F32),
        row_gather=pltpu.VMEM((tiles, row_count, channels), F32),
        count=pltpu.VMEM(line, F32),
        stat=pltpu.VMEM(line, F32),
        back=pltpu.VMEM(line, F32),
        slide_count=pltpu.VMEM(line, F32),
        count_gather=pltpu.VMEM((tiles,) + line, F32),
        stat_gather=pltpu.VMEM((tiles,) + line, F32),
        back_gather=pltpu.VMEM((tiles,) + line, F32),
        total_gather=pltpu.VMEM((slides,) + line, F32),
        edge_send=dma_sems(2, 2),
        edge_recv=dma_sems(2, 2),
        tile_send=dma_sems(4, tile_ends),
        tile_recv=dma_sems(4, tile_ends),
        slide_send=dma_sems(6, slide_ends),
        slide_recv=dma_sems(6, slide_ends),
        stage_send=dma_sems(4, bits),
        stage_recv=dma_sems(4, bits),
    )
    parts = {}
    for piece in range(4):
        span = 9 * channels if piece == 0 else 3 * channels
        parts[GRAD, piece, 0] = pltpu.VMEM((2,) * bits + (chunk, span), F32)
        plan = stage_plan(bits, order_of(bits, piece % 2 == 0))
        for stage, (_, _, left) in enumerate(plan):
            below = (2,) * left + (chunk, span)
            parts[RECV, piece, stage] = pltpu.VMEM(below, BF16 if stage else F32)
            if stage:
                parts[SEND, piece, stage] = pltpu.VMEM(below, BF16)
                parts[KEPT, piece, stage] = pltpu.VMEM(below, F32)
    names = list(inputs) + list(outputs) + list(scratch)
    final, heads, total = call(
        functools.partial(step_kernel, tiles, slides, bits, numbers, names, list(parts)),
        tuple(outputs.values()),
        list(scratch.values()) + list(parts.values()),
        tuple(inputs.values()),
        0,
    )
    loss, head, grads = call(
        functools.partial(finish_kernel, slides, classes),
        (
            shape_of((1, 1)),
            shape_of((4 + classes, channels)),
            shape_of((chunk, 9, 2, channels)),
        ),
        [],
        (final, heads, total),
    )
    return (loss[0, 0], head, grads.transpose(0, 2, 1, 3))


def solution(mesh):
    return jax.shard_map(
        per_device,
        mesh=mesh,
        in_specs=(
            P("slide", "tile", None, None),
            P("slide", "tile", None, None),
            P(),
            P(),
            P(),
            P(),
            P(),
            P(),
            P(),
            P(),
            P("slide", "tile", None),
        ),
        out_specs=(P(), P(), P("tile", None, None, None)),
        check_vma=False,
    )
```

time: 293 us -> 57 us (0.19)
  blocking collectives: 144 us -> 0 us
  waiting for transfers between devices: 59.7 us -> 0 us
  Pallas kernels: 0 us -> 56.2 us
  local copies, waits for them, and re-layouts: 28.9 us -> 0 us
  matrix products: 20 us -> 0 us
  between operations: 17.2 us -> 0.64 us
  other arithmetic: 11.3 us -> 0 us
  starting transfers between devices: 10.3 us -> 0 us
    psum x4 -> x0, blocking collectives: 144 us -> none  [the longest x1 40 us: per_device(): lax.psum((head_local, loss_local), ('slide', 'tile'))]
    reduce_scatter x1 -> x0, waiting for transfers between devices: 59.6 us -> none  [per_device(): lax.psum_scatter(whole, 'tile', scatter_dimension=0, tiled=True)]
    pallas_call x0 -> x2, Pallas kernels: none -> 56.2 us  [call(): pl.pallas_call(body, out_shape=out_shape, in_specs=[VMEM] * len(args), ou...]
    unnamed x96 -> x0, local copies, waits for them, and re-layouts: 21.5 us -> none
    dot_general x23 -> x0, matrix products: 20 us -> none  [the longest x2 7.89 us: per_device(): lax.dot_general(stacked, upstream, (((0,), (0,)), ((), ())), preferred_el...]
    ppermute x4 -> x0, starting transfers between devices: 10.2 us -> none  [the longest x2 7.66 us: padded_2(): lax.ppermute(tail, axis, [(i, (i + 1) % count) for i in range(ends)])]
    reduce_sum x12 -> x0, other arithmetic: 7.09 us -> none  [the longest x9 3.73 us: group_sums(): return values.reshape(values.shape[0], groups, -1).sum(axis=(0, 2))]
  transfers between devices with their start and end apart: 6 -> 0, of which waited for: 1 -> 0; matrix products, arithmetic and copies ran while one was open for 5% -> 0% of each run, Pallas kernels for 0% -> 0%
where the time goes in v2:
time: 57 us; the launch traced here: 56.9 us
  Pallas kernels  56.2 us (99%)
  between operations  0.64 us (1%)
    pallas_call x2, Pallas kernels, call(): pl.pallas_call(body, out_shape=out_shape, in_specs=[VMEM] * len(args), ou...  56.2 us

profile of v2, /device:TPU:0, one launch (start us, length us, event | category | flops | bytes accessed | tf_op | source)
XLA Modules:
  0.0 56.9 jit_solution(6537161863110276564)
XLA Ops:
  0.6 54.5 %shard_map.130 = (f32[2,16,2304]{2,1,0:T(8,128)}, f32[2,16,128]{2,1,0:T(8,128)}, f32[1,128]{1,0:T(1,128)}) custom-call(bf16[8,256,256]{2,1,0:T(8,128)(2,1)} %bitcast.12, bf16[4,128,256]{2,1,0:T(8,128)(2,1)} %bitcast.15, bf16[9,256,128]{2,1,0:T(8,128)(2,1)} %bitcast.13, bf16[9,256,128]{2,1,0:T(8,128)(2,1)} %bitcast.14, f32[1,128]{1,0:T(1,128)} %bitcast.17, ...), custom_call_target="tpu_custom_call" | custom-call | tf_op jit(solution)/shard_map/pallas_call | solution.py:28
  55.1 1.7 %shard_map.131 = (f32[1,1]{1,0:T(1,128)}, f32[12,128]{1,0:T(8,128)}, f32[16,9,2,128]{3,2,1,0:T(2,128)}) custom-call(f32[2,16,2304]{2,1,0:T(8,128)} %get-tuple-element.9.final, f32[2,16,128]{2,1,0:T(8,128)} %get-tuple-element.10.heads, f32[1,128]{1,0:T(1,128)} %get-tuple-element.11.total), custom_call_target="tpu_custom_call" | custom-call | tf_op jit(solution)/shard_map/pallas_call | solution.py:28

commit v3 on v2

--- a/solution.py
+++ b/solution.py
@@ -39,10 +39,11 @@
     return jax.ShapeDtypeStruct(dims, dtype)
 
 
-def greet(peers):
+def greet(peers, meanwhile):
     barrier = pltpu.get_barrier_semaphore()
     for peer in peers:
         pl.semaphore_signal(barrier, inc=1, device_id=peer, device_id_type=MESH)
+    meanwhile()
     pl.semaphore_wait(barrier, len(peers))
 
 
@@ -136,6 +137,7 @@
 
 
 PACK = 2
+PIECES = 6
 GRAD, SEND, RECV, KEPT = range(4)
 
 
@@ -174,11 +176,16 @@
     fine_gain, fine_offset = ref.fine_gain[...], ref.fine_offset[...]
     coarse_gain, coarse_offset = ref.coarse_gain[...], ref.coarse_offset[...]
 
-    tissue_here = (labels[...] >= 0).astype(F32)
-    ref.count[...] = jnp.broadcast_to(
-        jnp.sum(tissue_here, axis=(0, 1), keepdims=True), ref.count.shape
-    )
-    greet(ring_peers("tile", tiles) + ring_peers("slide", slides))
+    def prepare():
+        tissue_here = (labels[...] >= 0).astype(F32)
+        ref.count[...] = jnp.broadcast_to(
+            jnp.sum(tissue_here, axis=(0, 1), keepdims=True), ref.count.shape
+        )
+        sums[...] = jnp.zeros_like(sums)
+        fine_pad[pl.ds(1, height)] = fine[...]
+        coarse_pad[pl.ds(1, height // 2)] = coarse[...]
+
+    greet(ring_peers("tile", tiles) + ring_peers("slide", slides), prepare)
 
     def edge_copies(peer, down):
         return [
@@ -238,9 +245,6 @@
         for padded in (fine_pad, coarse_pad):
             padded[padded.shape[0] - 1] = jnp.zeros(padded.shape[1:], BF16)
 
-    sums[...] = jnp.zeros_like(sums)
-    fine_pad[pl.ds(1, height)] = fine[...]
-    coarse_pad[pl.ds(1, height // 2)] = coarse[...]
     fine_steps, coarse_steps = height // PACK, height // 2 // PACK
 
     @pl.loop(1, fine_steps - 1)
@@ -365,10 +369,8 @@
     ref.back[...] = packed_groups(rows[0:8] * gains, channels)
     back_copies = tile_copies(2, ref.back, ref.back_gather)
     start(back_copies)
-    row_copies = tile_copies(3, rows, ref.row_gather)
-    start(row_copies)
     ref.back_gather[me] = ref.back[...]
-    ref.row_gather[me] = rows[...]
+    ref.row_sums[0] = rows[...]
     wait(back_copies)
     back = unpacked_groups(ordered_sum(ref.back_gather, tiles), channels)
 
@@ -393,10 +395,10 @@
 
     mine = [lax.rem(me // (2**bit), 2) for bit in range(bits)]
     partners = [{"tile": me + (1 - 2 * mine[bit]) * (2**bit)} for bit in range(bits)]
-    plans = [stage_plan(bits, order_of(bits, piece % 2 == 0)) for piece in range(4)]
+    plans = [stage_plan(bits, order_of(bits, piece % 2)) for piece in range(PIECES)]
     final = ref.final
-    total_taps = 9 * channels
-    spans = [(total_taps, total_taps)] + [(a * 3 * channels, 3 * channels) for a in range(3)]
+    across = 3 * channels
+    spans = [((piece + 3) % PIECES * across, across) for piece in range(PIECES)]
 
     def buffer(piece, stage, kind):
         return ref.parts[kind, piece, stage]
@@ -430,7 +432,7 @@
             for d in range(1, slides)
         ]
 
-    done = [0] * 4
+    done = [0] * PIECES
 
     def advance(piece):
         stage = done[piece]
@@ -464,36 +466,53 @@
             turned[:, a * span : a * span + pixels], shifted[...], preferred_element_type=F32
         )
 
-    coarse_shifted, fine_shifted = ref.coarse_shifted, ref.fine_shifted
+    def row_copy(stage):
+        return pltpu.make_async_remote_copy(
+            src_ref=ref.row_sums.at[stage],
+            dst_ref=ref.row_gather.at[stage],
+            send_sem=ref.row_send.at[stage],
+            recv_sem=ref.row_recv.at[stage],
+            device_id=partners[stage],
+            device_id_type=MESH,
+        )
+
+    head_copies = slide_copies(1, ref.row_sums.at[bits], ref.head_gather)
+
+    def advance_rows(stage):
+        row_copy(stage).wait()
+        ref.row_sums[stage + 1] = ref.row_sums[stage] + ref.row_gather[stage]
+        if stage + 1 < bits:
+            row_copy(stage + 1).start()
+        else:
+            start(head_copies)
+            ref.head_gather[slide] = ref.row_sums[bits]
+
+    def begin(piece, turned, shifted, a, span):
+        out = ref.parts[GRAD, piece, 0]
+        out[...] = product(turned, shifted, a, span).reshape(out.shape)
+        stage_copy(piece, 0).start()
+
+    row_copy(0).start()
     upstream(coarse_conv, coarse_dpre, coarse_mean, coarse_scale, coarse_gain, 2, numbers[1],
-             half, coarse_shifted, coarse_steps)
-    lead = (slice(None),) * (bits + 1)
+             half, ref.coarse_shifted, coarse_steps)
     for a in range(3):
-        value = product(ref.coarse_turned, coarse_shifted, a, half)
-        out = ref.parts[GRAD, 0, 0]
-        out[lead + (slice(a * 3 * channels, (a + 1) * 3 * channels),)] = value.reshape(
-            out.shape[:-1] + (3 * channels,)
-        )
-    stage_copy(0, 0).start()
+        begin(a, ref.coarse_turned, ref.coarse_shifted, a, half)
     upstream(fine_conv, fine_dpre, fine_mean, fine_scale, fine_gain, 0, numbers[0],
-             width, fine_shifted, fine_steps)
-    for a in range(3):
-        out = ref.parts[GRAD, a + 1, 0]
-        out[...] = product(ref.fine_turned, fine_shifted, a, width).reshape(out.shape)
-        stage_copy(a + 1, 0).start()
-        if a < 2:
-            for piece in range(a + 1):
-                advance(piece)
-    wait(row_copies)
-    ref.slide_rows[...] = ordered_sum(ref.row_gather, tiles)
-    head_copies = slide_copies(1, ref.slide_rows, ref.head_gather)
-    start(head_copies)
-    ref.head_gather[slide] = ref.slide_rows[...]
-    while min(done) < bits:
-        for piece in range(4):
+             width, ref.fine_shifted, fine_steps)
+    advance(0)
+    begin(3, ref.fine_turned, ref.fine_shifted, 0, width)
+    advance(1)
+    begin(4, ref.fine_turned, ref.fine_shifted, 1, width)
+    advance(2)
+    begin(5, ref.fine_turned, ref.fine_shifted, 2, width)
+    for stage in range(bits):
+        for piece in range(PIECES // 2):
+            advance(piece)
+        advance_rows(stage)
+        for piece in range(PIECES // 2, PIECES):
             advance(piece)
     wait(head_copies)
-    for piece in range(4):
+    for piece in range(PIECES):
         wait(piece_copies(piece))
 
 
@@ -569,8 +588,10 @@
         fold=pltpu.VMEM((width, channels), F32),
         sums=pltpu.VMEM((8, channels), F32),
         rows=pltpu.VMEM((row_count, channels), F32),
-        slide_rows=pltpu.VMEM((row_count, channels), F32),
-        row_gather=pltpu.VMEM((tiles, row_count, channels), F32),
+        row_sums=pltpu.VMEM((bits + 1, row_count, channels), F32),
+        row_gather=pltpu.VMEM((bits, row_count, channels), F32),
+        row_send=dma_sems(bits),
+        row_recv=dma_sems(bits),
         count=pltpu.VMEM(line, F32),
         stat=pltpu.VMEM(line, F32),
         back=pltpu.VMEM(line, F32),
@@ -581,18 +602,18 @@
         total_gather=pltpu.VMEM((slides,) + line, F32),
         edge_send=dma_sems(2, 2),
         edge_recv=dma_sems(2, 2),
-        tile_send=dma_sems(4, tile_ends),
-        tile_recv=dma_sems(4, tile_ends),
-        slide_send=dma_sems(6, slide_ends),
-        slide_recv=dma_sems(6, slide_ends),
-        stage_send=dma_sems(4, bits),
-        stage_recv=dma_sems(4, bits),
+        tile_send=dma_sems(3, tile_ends),
+        tile_recv=dma_sems(3, tile_ends),
+        slide_send=dma_sems(2 + PIECES, slide_ends),
+        slide_recv=dma_sems(2 + PIECES, slide_ends),
+        stage_send=dma_sems(PIECES, bits),
+        stage_recv=dma_sems(PIECES, bits),
     )
     parts = {}
-    for piece in range(4):
-        span = 9 * channels if piece == 0 else 3 * channels
+    span = 3 * channels
+    for piece in range(PIECES):
         parts[GRAD, piece, 0] = pltpu.VMEM((2,) * bits + (chunk, span), F32)
-        plan = stage_plan(bits, order_of(bits, piece % 2 == 0))
+        plan = stage_plan(bits, order_of(bits, piece % 2))
         for stage, (_, _, left) in enumerate(plan):
             below = (2,) * left + (chunk, span)
             parts[RECV, piece, stage] = pltpu.VMEM(below, BF16 if stage else F32)

time: 57 us -> 51.1 us (0.90)
  Pallas kernels: 56.2 us -> 50.3 us
    pallas_call x2, Pallas kernels: 56.2 us -> 50.3 us  [call(): pl.pallas_call(body, out_shape=out_shape, in_specs=[VMEM] * len(args), ou...]
where the time goes in v3:
time: 51.1 us; the launch traced here: 50.9 us
  Pallas kernels  50.3 us (98%)
  between operations  0.64 us (1%)
    pallas_call x2, Pallas kernels, call(): pl.pallas_call(body, out_shape=out_shape, in_specs=[VMEM] * len(args), ou...  50.3 us

profile of v3, /device:TPU:0, one launch (start us, length us, event | category | flops | bytes accessed | tf_op | source)
XLA Modules:
  0.0 50.9 jit_solution(14143620055490702197)
XLA Ops:
  0.6 48.5 %shard_map.130 = (f32[2,16,2304]{2,1,0:T(8,128)}, f32[2,16,128]{2,1,0:T(8,128)}, f32[1,128]{1,0:T(1,128)}) custom-call(bf16[8,256,256]{2,1,0:T(8,128)(2,1)} %bitcast.12, bf16[4,128,256]{2,1,0:T(8,128)(2,1)} %bitcast.15, bf16[9,256,128]{2,1,0:T(8,128)(2,1)} %bitcast.13, bf16[9,256,128]{2,1,0:T(8,128)(2,1)} %bitcast.14, f32[1,128]{1,0:T(1,128)} %bitcast.17, ...), custom_call_target="tpu_custom_call" | custom-call | tf_op jit(solution)/shard_map/pallas_call | solution.py:28
  49.2 1.7 %shard_map.131 = (f32[1,1]{1,0:T(1,128)}, f32[12,128]{1,0:T(8,128)}, f32[16,9,2,128]{3,2,1,0:T(2,128)}) custom-call(f32[2,16,2304]{2,1,0:T(8,128)} %get-tuple-element.9.final, f32[2,16,128]{2,1,0:T(8,128)} %get-tuple-element.10.heads, f32[1,128]{1,0:T(1,128)} %get-tuple-element.11.total), custom_call_target="tpu_custom_call" | custom-call | tf_op jit(solution)/shard_map/pallas_call | solution.py:28
